TPU v7x, 256 devices: a whole 4x4x8 slice. The times are simulated.
256 devices in a mesh: dp: 32 (over z, y), ctx: 8 (over x, core).
Axes of the slice: x: 4, y: 4, z: 8, core: 2. Of those that a mesh axis runs over, the one named last changes fastest.
Arguments:
- query_rows: bfloat16 [32768, 4096], P(('dp', 'ctx')), may hold values from -9 to 9
- key_rows: bfloat16 [32768, 1024], P(('dp', 'ctx')), may hold values from -4 to 4
- token_values: bfloat16 [32768, 1024], P(('dp', 'ctx')), may hold values from -6 to 6
- group_of_row: int32 [32768, 1], P(('dp', 'ctx')), may hold values from 0 to 31; in each aligned block of 128 rows (0 to 127, 128 to 255, ...) at most 8 rows name the same one
- doc_lengths: int32 [32, 2], P('dp'), may hold values from 1 to 1536, 2048 in all within a row
Outputs:
- attended: bfloat16 [32768, 4096], P(('dp', 'ctx'))
Inputs may be any that keep to these rules, and one draw needn't show every extreme that they name: `group_of_row`: within each device's block of 128 rows no group is named by more than 8 rows; in some blocks one group is named by exactly 8. `doc_lengths`: each group's 2 lengths sum to 2048; neither exceeds 1536.
All inputs are finite; a program needn't handle non-finite values.
Results may differ from a plain program's by a relative error of at most 0.0038.
Values may be sent and summed in bfloat16 or wider, within the bound.
No kernel may reach another device: no remote copies, remote signals or barrier semaphores. Data moves between devices by JAX's collectives and lax.ppermute only.
A program may use at most 128 MiB of HBM per device.

v0:
```python
import math
import jax
import jax.numpy as jnp
from jax import lax
from jax.sharding import PartitionSpec as P

QUERY_HEAD_COUNT = 32
KEY_VALUE_HEADS = 8
HEAD_SIZE = 128
masked_score = -1e30


def rank_rows(indices):
    count_all = indices.shape[0]
    rows_per_block = 128
    usable = indices >= 0

    def count_before(pieces):
        earlier = usable[None, :] & (indices[None, :] < pieces[:, None])
        return jnp.sum(earlier.astype(jnp.int32), axis=1)

    counted = lax.map(count_before, indices.reshape(count_all // rows_per_block, rows_per_block))
    return counted.reshape(count_all)


def document_ids(ranks, starts):
    return jnp.sum((starts[None, :] <= ranks[:, None]).astype(jnp.int32), axis=1) - 1


def attend(block_of_queries, key_heads, value_heads, query_index, query_doc, key_index, key_doc):
    head_dim = key_heads.shape[2]
    scores = jnp.einsum(
        "qjgd,kjd->jgqk", block_of_queries, key_heads, preferred_element_type=jnp.float32
    )
    scores = scores * (1.0 / math.sqrt(head_dim))
    allowed = (
        (query_doc[:, None] == key_doc[None, :])
        & (key_index[None, :] <= query_index[:, None])
        & (key_index[None, :] >= 0)
    )
    scores = jnp.where(allowed[None, None], scores, masked_score)
    row_max = jnp.max(scores, axis=3, keepdims=True)
    weights = jnp.exp(scores - row_max)
    totals = jnp.sum(weights, axis=3)
    output = jnp.einsum(
        "jgqk,kjd->qjgd",
        weights.astype(jnp.bfloat16),
        value_heads,
        preferred_element_type=jnp.float32,
    )
    output = output / jnp.transpose(totals, (2, 0, 1))[..., None]
    return output.reshape(
        output.shape[0], output.shape[1], output.shape[2] * output.shape[3]
    ).astype(jnp.bfloat16)


def attend_all(query_heads, query_index, query_doc, key_heads, value_heads, key_index, key_doc):
    count_q = query_heads.shape[0]
    rows_per_block = min(128, count_q)
    blocks = count_q // rows_per_block

    def one_block(inputs_block):
        return attend(
            inputs_block[0],
            key_heads,
            value_heads,
            inputs_block[1],
            inputs_block[2],
            key_index,
            key_doc,
        )

    shaped = (
        query_heads.reshape((blocks, rows_per_block) + query_heads.shape[1:]),
        query_index.reshape(blocks, rows_per_block),
        query_doc.reshape(blocks, rows_per_block),
    )
    result = lax.map(one_block, shaped)
    return result.reshape((count_q,) + result.shape[2:])


def body(query_rows, key_rows, token_values, group_of_row, doc_lengths):
    dp_count = lax.axis_size("dp")
    tok_rows = query_rows.shape[0]
    slot_rows = 2 * tok_rows // dp_count
    key_value_head_count = KEY_VALUE_HEADS
    head_dim = HEAD_SIZE
    rows_per_group = QUERY_HEAD_COUNT // KEY_VALUE_HEADS
    group_ids = group_of_row[:, 0]
    onehot = (group_ids[:, None] == jnp.arange(dp_count, dtype=jnp.int32)[None, :]).astype(
        jnp.int32
    )
    position = jnp.sum((jnp.cumsum(onehot, axis=0) - onehot) * onehot, axis=1)
    target = group_ids * slot_rows + position
    stream = lax.axis_index(("dp", "ctx")) * tok_rows + jnp.arange(tok_rows, dtype=jnp.int32)
    send_count = dp_count * slot_rows
    send_query = (
        jnp.zeros((send_count, query_rows.shape[1]), jnp.bfloat16).at[target].set(query_rows)
    )
    send_key = jnp.zeros((send_count, key_rows.shape[1]), jnp.bfloat16).at[target].set(key_rows)
    send_value = (
        jnp.zeros((send_count, token_values.shape[1]), jnp.bfloat16).at[target].set(token_values)
    )
    send_index = jnp.full((send_count,), -1, jnp.int32).at[target].set(stream)
    arrived = (
        lax.all_to_all(
            send_query.reshape(dp_count, slot_rows, query_rows.shape[1]),
            "dp",
            split_axis=0,
            concat_axis=0,
            tiled=True,
        ),
        lax.all_to_all(
            send_key.reshape(dp_count, slot_rows, key_rows.shape[1]),
            "dp",
            split_axis=0,
            concat_axis=0,
            tiled=True,
        ),
        lax.all_to_all(
            send_value.reshape(dp_count, slot_rows, token_values.shape[1]),
            "dp",
            split_axis=0,
            concat_axis=0,
            tiled=True,
        ),
        lax.all_to_all(
            send_index.reshape(dp_count, slot_rows), "dp", split_axis=0, concat_axis=0, tiled=True
        ),
    )
    local_query = arrived[0].reshape(send_count, key_value_head_count, rows_per_group * head_dim)
    local_key = arrived[1].reshape(send_count, key_value_head_count, head_dim)
    local_value = arrived[2].reshape(send_count, key_value_head_count, head_dim)
    local_index = arrived[3].reshape(send_count)
    lengths = doc_lengths[0]
    starts = jnp.cumsum(lengths) - lengths
    group_key, group_value, group_index = (
        lax.all_gather(local_key, "ctx", axis=0, tiled=True),
        lax.all_gather(local_value, "ctx", axis=0, tiled=True),
        lax.all_gather(local_index, "ctx", axis=0, tiled=True),
    )
    group_doc = document_ids(rank_rows(group_index), starts)
    own_doc = lax.dynamic_slice_in_dim(group_doc, lax.axis_index("ctx") * send_count, send_count, 0)
    result = attend_all(
        local_query.reshape(send_count, key_value_head_count, rows_per_group, head_dim),
        local_index,
        own_doc,
        group_key,
        group_value,
        group_index,
        group_doc,
    )
    back_rows = result.reshape(send_count, key_value_head_count * rows_per_group * head_dim)
    returned = lax.all_to_all(
        back_rows.reshape(dp_count, slot_rows, back_rows.shape[1]),
        "dp",
        split_axis=0,
        concat_axis=0,
        tiled=True,
    )
    return returned.reshape(send_count, back_rows.shape[1])[target]


def solution(mesh):
    in_specs = (
        P(("dp", "ctx"), None),
        P(("dp", "ctx"), None),
        P(("dp", "ctx"), None),
        P(("dp", "ctx"), None),
        P("dp", None),
    )
    out_specs = P(("dp", "ctx"), None)
    return jax.shard_map(body, mesh=mesh, in_specs=in_specs, out_specs=out_specs, check_vma=False)
```

profile of v0, /device:TPU:8, one launch (start us, length us, event | category | flops | bytes accessed | tf_op | source)
XLA Modules:
  0.0 317.4 jit_solution(16999272624418811626)
XLA Ops:
  6.5 0.7 fusion.24
  7.5 0.8 select_reduce_fusion
  8.3 0.7 fusion.26
  9.0 1.7 scatter_custom_fusion.2
  10.7 28.3 %all_to_all.29 = bf16[32,8,1024]{2,1,0:T(8,128)(2,1)S(1)} all-to-all(bf16[32,8,1024]{2,1,0:T(8,128)(2,1)S(1)} %bitcast.108), channel_id=1, replica_groups=mesh['dp'=32,'ctx'=8] {'dp'}, dimensions={0} | all-to-all | bytes 1048576 | tf_op jit(solution)/shard_map/all_to_all | solution.py:113
  39.0 0.9 copy.26
  40.0 1.7 scatter_custom_fusion.3
  41.7 21.3 %all_to_all.30 = bf16[32,8,1024]{2,1,0:T(8,128)(2,1)S(1)} all-to-all(bf16[32,8,1024]{2,1,0:T(8,128)(2,1)S(1)} %bitcast.109), channel_id=1, replica_groups=mesh['dp'=32,'ctx'=8] {'dp'}, dimensions={0} | all-to-all | bytes 1048576 | tf_op jit(solution)/shard_map/all_to_all | solution.py:120
  63.1 0.9 copy.27
  64.0 1.0 scatter_custom_fusion
  65.0 0.7 all_to_all.18
  65.7 5.6 %all-to-all-start = ((s32[32,1,8]{2,1,0:T(1,128)}), s32[32,1,8]{2,1,0:T(1,128)S(1)}, u32[]{:S(2)}, u32[]{:S(2)}) async-start(s32[32,1,8]{2,1,0:T(1,128)} %bitcast.17), calls=%async_computation | async-start | bytes 32768 | tf_op jit(solution)/shard_map/all_to_all | solution.py:127
  71.5 4.4 %scatter_custom_fusion.1 = bf16[256,4096]{1,0:T(8,128)(2,1)} fusion(s32[128]{0:T(128)S(1)} %fusion.26, bf16[128,4096]{1,0:T(8,128)(2,1)} %param.9, bf16[]{:T(256)} %constant.33.clone.1), kind=kCustom, calls=%fused_computation.31 | custom fusion | bytes 2097664 | tf_op jit(solution)/shard_map/scatter | solution.py:98
  75.8 4.0 %all-to-all-done = s32[32,1,8]{2,1,0:T(1,128)S(1)} async-done(((s32[32,1,8]{2,1,0:T(1,128)}), s32[32,1,8]{2,1,0:T(1,128)S(1)}, u32[]{:S(2)}, u32[]{:S(2)}) %all-to-all-start) | async-done | bytes 1056 | tf_op jit(solution)/shard_map/all_to_all | solution.py:127
  79.8 5.8 %all-to-all-start.1 = ((bf16[32,8,4096]{2,1,0:T(8,128)(2,1)}), bf16[32,8,4096]{2,1,0:T(8,128)(2,1)S(1)}, u32[]{:S(2)}, u32[]{:S(2)}) async-start(bf16[32,8,4096]{2,1,0:T(8,128)(2,1)} %bitcast.22), calls=%async_computation.1 | async-start | bytes 4194304 | tf_op jit(solution)/shard_map/all_to_all | solution.py:106
  85.6 0.5 broadcast.116
  86.2 0.7 reduce.5
  87.0 11.0 %all-gather = s32[8,1,256]{2,1,0:T(1,128)S(1)} all-gather(s32[1,1,256]{2,1,0:T(1,128)S(1)} %reshape.188), channel_id=1, replica_groups=mesh['dp'=32,'ctx'=8] {'ctx'}, dimensions={0}, use_global_device_ids=true | all-gather | bytes 9216 | tf_op jit(solution)/shard_map/all_gather | solution.py:140
  98.1 5.6 %while.20 = (s32[]{:T(128)}, s32[16,128]{1,0:T(8,128)S(1)}, pred[2048]{0:T(1024)(128)(4,1)S(1)}, s32[2048]{0:T(1024)S(1)}, s32[16,128]{1,0:T(8,128)S(1)}, /*index=5*/s32[]{:T(128)}, s32[]{:T(128)}) while((s32[]{:T(128)}, s32[16,128]{1,0:T(8,128)S(1)}, pred[2048]{0:T(1024)(128)(4,1)S(1)}, s32[2048]{0:T(1024)S(1)}, s32[16,128]{1,0:T(8,128)S(1)}, ...), condition=%wide.region_7.8_spmd, body=%wide.region_5.7_spmd.sunk | while | flops 1048450 | bytes 13397 | solution.py:22
  98.1 0.3 convert_reduce_fusion.2
  98.4 0.3 convert_reduce_fusion.2
  98.8 0.3 convert_reduce_fusion.2
  99.1 0.3 convert_reduce_fusion.2
  99.5 0.3 convert_reduce_fusion.2
  99.8 0.3 convert_reduce_fusion.2
  103.8 30.9 %all-to-all-done.1 = bf16[32,8,4096]{2,1,0:T(8,128)(2,1)S(1)} async-done(((bf16[32,8,4096]{2,1,0:T(8,128)(2,1)}), bf16[32,8,4096]{2,1,0:T(8,128)(2,1)S(1)}, u32[]{:S(2)}, u32[]{:S(2)}) %all-to-all-start.1) | async-done | bytes 2097184 | tf_op jit(solution)/shard_map/all_to_all | solution.py:106
  134.8 2.7 reshape_reshape_reshape.6
  137.5 4.8 %copy.18 = bf16[2048,8,128]{2,0,1:T(8,128)(2,1)} copy(bf16[2048,8,128]{2,1,0:T(8,128)(2,1)} %all-gather.4.cloned.1.call-done) | data formatting | bytes 8388608 | tf_op jit(solution)/shard_map/while | solution.py:78
  142.2 6.7 %copy.19 = bf16[2048,8,128]{0,2,1:T(8,128)(2,1)} copy(bf16[2048,8,128]{2,1,0:T(8,128)(2,1)} %all-gather.6.cloned.1.call-done) | data formatting | bytes 8388608 | tf_op jit(solution)/shard_map/while | solution.py:78
  148.9 102.2 %while.21 = (s32[]{:T(128)}, bf16[2,128,8,512]{3,2,1,0:T(8,128)(2,1)}, s32[2,128]{1,0:T(2,128)S(1)}, s32[2048]{0:T(1024)S(1)}, s32[2048]{0:T(1024)S(1)}, /*index...) while((s32[]{:T(128)}, ...), condition=%wide.region_14.15_spmd, body=%wide.region_11.14_spmd.sunk | while | flops 4389332992 | bytes 118603368 | solution.py:78
  148.9 0.3 and_and_fusion.2
  149.3 1.6 constant_dynamic-slice_fusion.4
  150.9 16.3 %bitcast_reduce_fusion.2 = (f32[8,4,128]{2,1,0:T(4,128)S(1)}, f32[8,128,4,2048]{3,1,2,0:T(8,128)}) fusion(pred[128,2048]{1,0:T(8,128)(4,1)S(1)} %and_and_fusion.2, bf16[2048,8,128]{2,0,1:T(8,128)(2,1)} %get-tuple-element.282, bf16[1,128,8,4,128]{4,3,2,1,0:T(4,128)(2,1)S(1)} %constant_dynamic-slice_fusion.4), kind=kOutput, calls=%fused_computation.8.clone.1 | convolution fusion | flops 2172645376 | bytes 39075840 | tf_op jit(solution)/shard_map/while/body/eval_jaxpr/qjgd,kjd->jgqk/dot_general | solution.py:32
  167.1 15.0 %fusion.37 = f32[8,4,128]{2,1,0:T(4,128)S(1)} fusion(f32[8,128,4,2048]{3,1,2,0:T(8,128)} %get-tuple-element.232, f32[8,4,128]{2,1,0:T(4,128)S(1)} %get-tuple-element.233, pred[128,2048]{1,0:T(8,128)(4,1)S(1)} %and_and_fusion.2), kind=kLoop, calls=%fused_computation.11.clone.1 | loop fusion | flops 33550336 | bytes 33849344 | tf_op jit(solution)/shard_map/while/body/eval_jaxpr/reduce_sum | solution.py:44
  182.1 15.9 %fusion.38 = bf16[128,8,4,128]{0,3,2,1:T(8,128)(2,1)S(1)} fusion(bf16[2048,8,128]{0,2,1:T(8,128)(2,1)} %get-tuple-element.283, f32[8,128,4,2048]{3,1,2,0:T(8,128)} %get-tuple-element.232, f32[8,4,128]{2,1,0:T(4,128)S(1)} %get-tuple-element.233, pred[128,2048]{1,0:T(8,128)(4,1)S(1)} %and_and_fusion.2, f32[128,8,4]{0,2,1:T(4,128)S(1)} %bitcast.110), kind=kOutput, calls=%fused_computation.19.clone.1 | convolution fusion | flops 2182086656 | bytes 39092224 | tf_op jit(solution)/shard_map/while/body/eval_jaxpr/jgqk,kjd->qjgd/dot_general | solution.py:45
  198.0 0.9 copy.35
  198.9 1.1 constant_dynamic-update-slice_fusion.2
  200.0 0.3 and_and_fusion.2
  200.3 1.6 constant_dynamic-slice_fusion.4
  201.9 16.3 %bitcast_reduce_fusion.2 = (f32[8,4,128]{2,1,0:T(4,128)S(1)}, f32[8,128,4,2048]{3,1,2,0:T(8,128)}) fusion(pred[128,2048]{1,0:T(8,128)(4,1)S(1)} %and_and_fusion.2, bf16[2048,8,128]{2,0,1:T(8,128)(2,1)} %get-tuple-element.282, bf16[1,128,8,4,128]{4,3,2,1,0:T(4,128)(2,1)S(1)} %constant_dynamic-slice_fusion.4), kind=kOutput, calls=%fused_computation.8.clone.1 | convolution fusion | flops 2172645376 | bytes 39075840 | tf_op jit(solution)/shard_map/while/body/eval_jaxpr/qjgd,kjd->jgqk/dot_general | solution.py:32
  218.2 15.0 %fusion.37 = f32[8,4,128]{2,1,0:T(4,128)S(1)} fusion(f32[8,128,4,2048]{3,1,2,0:T(8,128)} %get-tuple-element.232, f32[8,4,128]{2,1,0:T(4,128)S(1)} %get-tuple-element.233, pred[128,2048]{1,0:T(8,128)(4,1)S(1)} %and_and_fusion.2), kind=kLoop, calls=%fused_computation.11.clone.1 | loop fusion | flops 33550336 | bytes 33849344 | tf_op jit(solution)/shard_map/while/body/eval_jaxpr/reduce_sum | solution.py:44
  233.2 15.9 %fusion.38 = bf16[128,8,4,128]{0,3,2,1:T(8,128)(2,1)S(1)} fusion(bf16[2048,8,128]{0,2,1:T(8,128)(2,1)} %get-tuple-element.283, f32[8,128,4,2048]{3,1,2,0:T(8,128)} %get-tuple-element.232, f32[8,4,128]{2,1,0:T(4,128)S(1)} %get-tuple-element.233, pred[128,2048]{1,0:T(8,128)(4,1)S(1)} %and_and_fusion.2, f32[128,8,4]{0,2,1:T(4,128)S(1)} %bitcast.110), kind=kOutput, calls=%fused_computation.19.clone.1 | convolution fusion | flops 2182086656 | bytes 39092224 | tf_op jit(solution)/shard_map/while/body/eval_jaxpr/jgqk,kjd->qjgd/dot_general | solution.py:45
  249.1 0.9 copy.35
  250.0 1.1 constant_dynamic-update-slice_fusion.2
  251.1 4.2 %reshape_reshape_reshape.7 = bf16[32,8,4096]{2,1,0:T(8,128)(2,1)} reshape(bf16[2,128,8,512]{3,2,1,0:T(8,128)(2,1)} %get-tuple-element.80) | data formatting | bytes 4194304 | tf_op jit(solution)/shard_map/reshape;reshape;reshape | solution.py:155
  255.3 5.6 %all-to-all-start.4 = ((bf16[32,8,4096]{2,1,0:T(8,128)(2,1)}), bf16[32,8,4096]{2,1,0:T(8,128)(2,1)S(1)}, u32[]{:S(2)}, u32[]{:S(2)}) async-start(bf16[32,8,4096]{2,1,0:T(8,128)(2,1)} %reshape_reshape_reshape.7), calls=%async_computation.4 | async-start | bytes 4194304 | tf_op jit(solution)/shard_map/all_to_all | solution.py:154
  260.9 47.5 %all-to-all-done.4 = bf16[32,8,4096]{2,1,0:T(8,128)(2,1)S(1)} async-done(((bf16[32,8,4096]{2,1,0:T(8,128)(2,1)}), bf16[32,8,4096]{2,1,0:T(8,128)(2,1)S(1)}, u32[]{:S(2)}, u32[]{:S(2)}) %all-to-all-start.4) | async-done | bytes 2097184 | tf_op jit(solution)/shard_map/all_to_all | solution.py:154
  308.4 2.2 gather_fusion
  (71 shorter events, 4.4 us)
Async XLA Ops:
  6.5 64.7 %copy-start.2 = (s32[1,2]{1,0:T(1,128)S(1)}, s32[1,2]{1,0:T(1,128)}, u32[]{:S(2)}) copy-start(s32[1,2]{1,0:T(1,128)} %param.13) | copy-start | bytes 28
  6.5 130.9 %all-gather.4.cloned.1.call-start = ((), (), s32[]{:S(2)}) async-start(), calls=%async_computation.5 | async-start | bytes 4718592 | tf_op jit(solution)/shard_map/all_gather | solution.py:138
  9.0 66.9 %copy-start = (s32[128]{0:T(128)}, s32[128]{0:T(128)S(1)}, u32[]{:S(2)}) copy-start(s32[128]{0:T(128)S(1)} %fusion.26) | copy-start | bytes 1540
  39.9 102.3 %all-gather.6.cloned.1.call-start = ((), (), s32[]{:S(2)}) async-start(), calls=%async_computation.6 | async-start | bytes 4718592 | tf_op jit(solution)/shard_map/all_gather | solution.py:139
  65.7 14.1 %all-to-all-start = ((s32[32,1,8]{2,1,0:T(1,128)}), s32[32,1,8]{2,1,0:T(1,128)S(1)}, u32[]{:S(2)}, u32[]{:S(2)}) async-start(s32[32,1,8]{2,1,0:T(1,128)} %bitcast.17), calls=%async_computation | async-start | bytes 32768 | tf_op jit(solution)/shard_map/all_to_all | solution.py:127
  79.8 55.0 %all-to-all-start.1 = ((bf16[32,8,4096]{2,1,0:T(8,128)(2,1)}), bf16[32,8,4096]{2,1,0:T(8,128)(2,1)S(1)}, u32[]{:S(2)}, u32[]{:S(2)}) async-start(bf16[32,8,4096]{2,1,0:T(8,128)(2,1)} %bitcast.22), calls=%async_computation.1 | async-start | bytes 4194304 | tf_op jit(solution)/shard_map/all_to_all | solution.py:106
  251.1 9.8 %copy-start.1 = (s32[128]{0:T(128)S(1)}, s32[128]{0:T(128)}, u32[]{:S(2)}) copy-start(s32[128]{0:T(128)} %copy-done) | copy-start | bytes 1540
  255.3 53.1 %all-to-all-start.4 = ((bf16[32,8,4096]{2,1,0:T(8,128)(2,1)}), bf16[32,8,4096]{2,1,0:T(8,128)(2,1)S(1)}, u32[]{:S(2)}, u32[]{:S(2)}) async-start(bf16[32,8,4096]{2,1,0:T(8,128)(2,1)} %reshape_reshape_reshape.7), calls=%async_computation.4 | async-start | bytes 4194304 | tf_op jit(solution)/shard_map/all_to_all | solution.py:154
Sparse Core Ops, SparseCore 0:
  40.1 31.3 all-gather.3
  73.3 34.5 all-gather.5
where the time goes:
time: 319 us; the launch traced here: 317 us
  waiting for transfers between devices  82.5 us (26%)
  matrix products  64.3 us (20%)
  blocking collectives  60.7 us (19%)
  local copies, waits for them, and re-layouts  40.5 us (13%)
  other arithmetic  38.6 us (12%)
  starting transfers between devices  17 us (5%)
  between operations  13.5 us (4%)
    all_to_all x1, waiting for transfers between devices, body(): lax.all_to_all(back_rows.reshape(dp_count, slot_rows, back_rows.shape[1])...  47.5 us
    dot_general x2, matrix products, attend(): jnp.einsum('qjgd,kjd->jgqk', block_of_queries, key_heads, preferred_eleme...  32.5 us
    dot_general x2, matrix products, attend(): jnp.einsum('jgqk,kjd->qjgd', weights.astype(jnp.bfloat16), value_heads, p...  31.8 us
    all_to_all x1, waiting for transfers between devices, body(): lax.all_to_all(send_query.reshape(dp_count, slot_rows, query_rows.shape[1...  30.9 us
    reduce_sum x2, other arithmetic, attend(): totals = jnp.sum(weights, axis=3)  30 us
    all_to_all x1, blocking collectives, body(): lax.all_to_all(send_key.reshape(dp_count, slot_rows, key_rows.shape[1]),...  28.3 us
    all_to_all x1, blocking collectives, body(): lax.all_to_all(send_value.reshape(dp_count, slot_rows, token_values.shape...  21.3 us
    while x2, local copies, waits for them, and re-layouts, attend_all(): result = lax.map(one_block, shaped)  11.5 us
  transfers between devices with their start and end apart: 5, of which 3 were waited for; matrix products, arithmetic and copies ran while one was open for 7% of the time, Pallas kernels for 0%

commit v1 on v0

--- a/solution.py
+++ b/solution.py
@@ -137,7 +137,9 @@
     group_key, group_value, group_index = (
         lax.all_gather(local_key, "ctx", axis=0, tiled=True),
         lax.all_gather(local_value, "ctx", axis=0, tiled=True),
-        lax.all_gather(local_index, "ctx", axis=0, tiled=True),
+        jnp.concatenate(
+            lax.all_to_all(jnp.stack([local_index] * lax.axis_size("ctx")), "ctx", 0, 0), axis=0
+        ),
     )
     group_doc = document_ids(rank_rows(group_index), starts)
     own_doc = lax.dynamic_slice_in_dim(group_doc, lax.axis_index("ctx") * send_count, send_count, 0)

time: 319 us -> 333 us (1.044)
  waiting for transfers between devices: 82.5 us -> 101 us
  blocking collectives: 60.7 us -> 49.7 us
  starting transfers between devices: 17 us -> 21.9 us
    all_to_all x1, waiting for transfers between devices: 30.9 us -> 43.7 us  [body(): lax.all_to_all(send_query.reshape(dp_count, slot_rows, query_rows.shape[1...]
    all_gather x1 -> x0, blocking collectives: 11 us -> none  [body(): lax.all_gather(local_index, 'ctx', axis=0, tiled=True)]
    all_to_all x1, waiting for transfers between devices: 3.97 us -> 8.36 us  [body(): lax.all_to_all(send_index.reshape(dp_count, slot_rows), 'dp', split_axis=...]
    all_to_all x0 -> x1, starting transfers between devices: none -> 4.3 us  [body(): lax.all_to_all(jnp.stack([local_index] * lax.axis_size('ctx')), 'ctx', 0, 0)]
  transfers between devices with their start and end apart: 5 -> 6, of which waited for: 3 -> 4; matrix products, arithmetic and copies ran while one was open for 7% -> 7% of each run, Pallas kernels for 0% -> 0%
where the time goes in v1:
time: 333 us; the launch traced here: 331 us
  waiting for transfers between devices  101 us (30%)
  matrix products  64.3 us (19%)
  blocking collectives  49.7 us (15%)
  local copies, waits for them, and re-layouts  41.3 us (12%)
  other arithmetic  38.6 us (12%)
  starting transfers between devices  21.9 us (7%)
  between operations  13.6 us (4%)
    all_to_all x1, waiting for transfers between devices, body(): lax.all_to_all(back_rows.reshape(dp_count, slot_rows, back_rows.shape[1])...  48.6 us
    all_to_all x1, waiting for transfers between devices, body(): lax.all_to_all(send_query.reshape(dp_count, slot_rows, query_rows.shape[1...  43.7 us
    dot_general x2, matrix products, attend(): jnp.einsum('qjgd,kjd->jgqk', block_of_queries, key_heads, preferred_eleme...  32.5 us
    dot_general x2, matrix products, attend(): jnp.einsum('jgqk,kjd->qjgd', weights.astype(jnp.bfloat16), value_heads, p...  31.8 us
    reduce_sum x2, other arithmetic, attend(): totals = jnp.sum(weights, axis=3)  30 us
    all_to_all x1, blocking collectives, body(): lax.all_to_all(send_key.reshape(dp_count, slot_rows, key_rows.shape[1]),...  28.3 us
    all_to_all x1, blocking collectives, body(): lax.all_to_all(send_value.reshape(dp_count, slot_rows, token_values.shape...  21.3 us
    while x2, local copies, waits for them, and re-layouts, attend_all(): result = lax.map(one_block, shaped)  11.5 us
  transfers between devices with their start and end apart: 6, of which 4 were waited for; matrix products, arithmetic and copies ran while one was open for 7% of the time, Pallas kernels for 0%

profile of v1, /device:TPU:8, one launch (start us, length us, event | category | flops | bytes accessed | tf_op | source)
XLA Modules:
  0.0 331.4 jit_solution(15419932694990189748)
XLA Ops:
  6.5 0.7 fusion.24
  7.5 0.8 select_reduce_fusion
  8.3 0.7 fusion.26
  9.0 1.7 scatter_custom_fusion.2
  10.7 28.3 %all_to_all.38 = bf16[32,8,1024]{2,1,0:T(8,128)(2,1)S(1)} all-to-all(bf16[32,8,1024]{2,1,0:T(8,128)(2,1)S(1)} %bitcast.116), channel_id=1, replica_groups=mesh['dp'=32,'ctx'=8] {'dp'}, dimensions={0} | all-to-all | bytes 1048576 | tf_op jit(solution)/shard_map/all_to_all | solution.py:113
  39.0 0.9 copy.33
  40.0 1.7 scatter_custom_fusion.3
  41.7 21.3 %all_to_all.39 = bf16[32,8,1024]{2,1,0:T(8,128)(2,1)S(1)} all-to-all(bf16[32,8,1024]{2,1,0:T(8,128)(2,1)S(1)} %bitcast.117), channel_id=1, replica_groups=mesh['dp'=32,'ctx'=8] {'dp'}, dimensions={0} | all-to-all | bytes 1048576 | tf_op jit(solution)/shard_map/all_to_all | solution.py:120
  63.1 0.9 copy.34
  64.0 1.0 scatter_custom_fusion
  65.0 0.7 all_to_all.24
  65.7 5.6 %all-to-all-start = ((s32[32,1,8]{2,1,0:T(1,128)}), s32[32,1,8]{2,1,0:T(1,128)S(1)}, u32[]{:S(2)}, u32[]{:S(2)}) async-start(s32[32,1,8]{2,1,0:T(1,128)} %bitcast.17), calls=%async_computation | async-start | bytes 32768 | tf_op jit(solution)/shard_map/all_to_all | solution.py:127
  71.4 8.4 %all-to-all-done = s32[32,1,8]{2,1,0:T(1,128)S(1)} async-done(((s32[32,1,8]{2,1,0:T(1,128)}), s32[32,1,8]{2,1,0:T(1,128)S(1)}, u32[]{:S(2)}, u32[]{:S(2)}) %all-to-all-start) | async-done | bytes 1056 | tf_op jit(solution)/shard_map/all_to_all | solution.py:127
  79.8 0.5 broadcast.121
  80.3 0.7 reduce.7
  81.1 0.6 stack.6
  81.7 4.3 %all-to-all-start.1 = ((s32[8,1,256]{2,1,0:T(1,128)}), s32[8,1,256]{2,1,0:T(1,128)S(1)}, u32[]{:S(2)}, u32[]{:S(2)}) async-start(s32[8,1,256]{2,1,0:T(1,128)} %stack.6), calls=%async_computation.1 | async-start | bytes 16384 | tf_op jit(solution)/shard_map/all_to_all | solution.py:141
  86.0 4.5 %scatter_custom_fusion.1 = bf16[256,4096]{1,0:T(8,128)(2,1)} fusion(s32[128]{0:T(128)S(1)} %fusion.26, bf16[128,4096]{1,0:T(8,128)(2,1)} %param.9, bf16[]{:T(256)} %constant.33.clone.1), kind=kCustom, calls=%fused_computation.31 | custom fusion | bytes 2097664 | tf_op jit(solution)/shard_map/scatter | solution.py:98
  90.6 0.8 all-to-all-done.1
  91.4 5.1 %all-to-all-start.2 = ((bf16[32,8,4096]{2,1,0:T(8,128)(2,1)}), bf16[32,8,4096]{2,1,0:T(8,128)(2,1)S(1)}, u32[]{:S(2)}, u32[]{:S(2)}) async-start(bf16[32,8,4096]{2,1,0:T(8,128)(2,1)} %bitcast.21), calls=%async_computation.2 | async-start | bytes 4194304 | tf_op jit(solution)/shard_map/all_to_all | solution.py:106
  96.6 5.8 %while.20 = (s32[]{:T(128)}, s32[16,128]{1,0:T(8,128)S(1)}, pred[2048]{0:T(1024)(128)(4,1)S(1)}, s32[8,256]{1,0:T(8,128)S(1)}, s32[16,128]{1,0:T(8,128)S(1)}, /*index=5*/s32[]{:T(128)}, s32[]{:T(128)}) while((s32[]{:T(128)}, s32[16,128]{1,0:T(8,128)S(1)}, pred[2048]{0:T(1024)(128)(4,1)S(1)}, s32[8,256]{1,0:T(8,128)S(1)}, ...), condition=%wide.region_7.8_spmd, body=%wide.region_5.7_spmd.sunk | while | flops 1048450 | bytes 29781 | solution.py:22
  97.0 0.3 convert_reduce_fusion.2
  98.5 0.3 convert_reduce_fusion.2
  100.3 0.3 convert_reduce_fusion.2
  102.1 0.3 convert_reduce_fusion.2
  102.6 43.7 %all-to-all-done.2 = bf16[32,8,4096]{2,1,0:T(8,128)(2,1)S(1)} async-done(((bf16[32,8,4096]{2,1,0:T(8,128)(2,1)}), bf16[32,8,4096]{2,1,0:T(8,128)(2,1)S(1)}, u32[]{:S(2)}, u32[]{:S(2)}) %all-to-all-start.2) | async-done | bytes 2097184 | tf_op jit(solution)/shard_map/all_to_all | solution.py:106
  146.3 2.7 reshape_reshape_reshape.6
  149.0 4.8 %copy.22 = bf16[2048,8,128]{2,0,1:T(8,128)(2,1)} copy(bf16[2048,8,128]{2,1,0:T(8,128)(2,1)} %all-gather.3.cloned.1.call-done) | data formatting | bytes 8388608 | tf_op jit(solution)/shard_map/while | solution.py:78
  153.7 6.7 %copy.23 = bf16[2048,8,128]{0,2,1:T(8,128)(2,1)} copy(bf16[2048,8,128]{2,1,0:T(8,128)(2,1)} %all-gather.5.cloned.1.call-done) | data formatting | bytes 8388608 | tf_op jit(solution)/shard_map/while | solution.py:78
  160.4 102.2 %while.21 = (s32[]{:T(128)}, bf16[2,128,8,512]{3,2,1,0:T(8,128)(2,1)}, s32[2,128]{1,0:T(2,128)S(1)}, s32[2048]{0:T(1024)S(1)}, s32[8,256]{1,0:T(8,128)S(1)}, /*i...) while((s32[]{:T(128)}, ...), condition=%wide.region_14.15_spmd, body=%wide.region_11.14_spmd.sunk | while | flops 4389332992 | bytes 118619752 | solution.py:78
  160.4 0.3 and_and_fusion.2
  160.8 1.6 constant_dynamic-slice_fusion.4
  162.4 16.3 %bitcast_reduce_fusion.2 = (f32[8,4,128]{2,1,0:T(4,128)S(1)}, f32[8,128,4,2048]{3,1,2,0:T(8,128)}) fusion(pred[128,2048]{1,0:T(8,128)(4,1)S(1)} %and_and_fusion.2, bf16[2048,8,128]{2,0,1:T(8,128)(2,1)} %get-tuple-element.291, bf16[1,128,8,4,128]{4,3,2,1,0:T(4,128)(2,1)S(1)} %constant_dynamic-slice_fusion.4), kind=kOutput, calls=%fused_computation.8.clone.1 | convolution fusion | flops 2172645376 | bytes 39075840 | tf_op jit(solution)/shard_map/while/body/eval_jaxpr/qjgd,kjd->jgqk/dot_general | solution.py:32
  178.6 15.0 %fusion.37 = f32[8,4,128]{2,1,0:T(4,128)S(1)} fusion(f32[8,128,4,2048]{3,1,2,0:T(8,128)} %get-tuple-element.241, f32[8,4,128]{2,1,0:T(4,128)S(1)} %get-tuple-element.242, pred[128,2048]{1,0:T(8,128)(4,1)S(1)} %and_and_fusion.2), kind=kLoop, calls=%fused_computation.11.clone.1 | loop fusion | flops 33550336 | bytes 33849344 | tf_op jit(solution)/shard_map/while/body/eval_jaxpr/reduce_sum | solution.py:44
  193.6 15.9 %fusion.38 = bf16[128,8,4,128]{0,3,2,1:T(8,128)(2,1)S(1)} fusion(bf16[2048,8,128]{0,2,1:T(8,128)(2,1)} %get-tuple-element.292, f32[8,128,4,2048]{3,1,2,0:T(8,128)} %get-tuple-element.241, f32[8,4,128]{2,1,0:T(4,128)S(1)} %get-tuple-element.242, pred[128,2048]{1,0:T(8,128)(4,1)S(1)} %and_and_fusion.2, f32[128,8,4]{0,2,1:T(4,128)S(1)} %bitcast.124), kind=kOutput, calls=%fused_computation.19.clone.1 | convolution fusion | flops 2182086656 | bytes 39092224 | tf_op jit(solution)/shard_map/while/body/eval_jaxpr/jgqk,kjd->qjgd/dot_general | solution.py:45
  209.5 0.9 copy.48
  210.4 1.1 constant_dynamic-update-slice_fusion.2
  211.5 0.3 and_and_fusion.2
  211.9 1.6 constant_dynamic-slice_fusion.4
  213.5 16.3 %bitcast_reduce_fusion.2 = (f32[8,4,128]{2,1,0:T(4,128)S(1)}, f32[8,128,4,2048]{3,1,2,0:T(8,128)}) fusion(pred[128,2048]{1,0:T(8,128)(4,1)S(1)} %and_and_fusion.2, bf16[2048,8,128]{2,0,1:T(8,128)(2,1)} %get-tuple-element.291, bf16[1,128,8,4,128]{4,3,2,1,0:T(4,128)(2,1)S(1)} %constant_dynamic-slice_fusion.4), kind=kOutput, calls=%fused_computation.8.clone.1 | convolution fusion | flops 2172645376 | bytes 39075840 | tf_op jit(solution)/shard_map/while/body/eval_jaxpr/qjgd,kjd->jgqk/dot_general | solution.py:32
  229.7 15.0 %fusion.37 = f32[8,4,128]{2,1,0:T(4,128)S(1)} fusion(f32[8,128,4,2048]{3,1,2,0:T(8,128)} %get-tuple-element.241, f32[8,4,128]{2,1,0:T(4,128)S(1)} %get-tuple-element.242, pred[128,2048]{1,0:T(8,128)(4,1)S(1)} %and_and_fusion.2), kind=kLoop, calls=%fused_computation.11.clone.1 | loop fusion | flops 33550336 | bytes 33849344 | tf_op jit(solution)/shard_map/while/body/eval_jaxpr/reduce_sum | solution.py:44
  244.7 15.9 %fusion.38 = bf16[128,8,4,128]{0,3,2,1:T(8,128)(2,1)S(1)} fusion(bf16[2048,8,128]{0,2,1:T(8,128)(2,1)} %get-tuple-element.292, f32[8,128,4,2048]{3,1,2,0:T(8,128)} %get-tuple-element.241, f32[8,4,128]{2,1,0:T(4,128)S(1)} %get-tuple-element.242, pred[128,2048]{1,0:T(8,128)(4,1)S(1)} %and_and_fusion.2, f32[128,8,4]{0,2,1:T(4,128)S(1)} %bitcast.124), kind=kOutput, calls=%fused_computation.19.clone.1 | convolution fusion | flops 2182086656 | bytes 39092224 | tf_op jit(solution)/shard_map/while/body/eval_jaxpr/jgqk,kjd->qjgd/dot_general | solution.py:45
  260.6 0.9 copy.48
  261.5 1.1 constant_dynamic-update-slice_fusion.2
  262.6 4.2 %reshape_reshape_reshape.7 = bf16[32,8,4096]{2,1,0:T(8,128)(2,1)} reshape(bf16[2,128,8,512]{3,2,1,0:T(8,128)(2,1)} %get-tuple-element.80) | data formatting | bytes 4194304 | tf_op jit(solution)/shard_map/reshape;reshape;reshape | solution.py:157
  266.8 6.9 %all-to-all-start.5 = ((bf16[32,8,4096]{2,1,0:T(8,128)(2,1)}), bf16[32,8,4096]{2,1,0:T(8,128)(2,1)S(1)}, u32[]{:S(2)}, u32[]{:S(2)}) async-start(bf16[32,8,4096]{2,1,0:T(8,128)(2,1)} %reshape_reshape_reshape.7), calls=%async_computation.5 | async-start | bytes 4194304 | tf_op jit(solution)/shard_map/all_to_all | solution.py:156
  273.7 48.6 %all-to-all-done.5 = bf16[32,8,4096]{2,1,0:T(8,128)(2,1)S(1)} async-done(((bf16[32,8,4096]{2,1,0:T(8,128)(2,1)}), bf16[32,8,4096]{2,1,0:T(8,128)(2,1)S(1)}, u32[]{:S(2)}, u32[]{:S(2)}) %all-to-all-start.5) | async-done | bytes 2097184 | tf_op jit(solution)/shard_map/all_to_all | solution.py:156
  322.4 2.2 gather_fusion
  (93 shorter events, 5.1 us)
Async XLA Ops:
  6.5 64.7 %copy-start.2 = (s32[1,2]{1,0:T(1,128)S(1)}, s32[1,2]{1,0:T(1,128)}, u32[]{:S(2)}) copy-start(s32[1,2]{1,0:T(1,128)} %param.13) | copy-start | bytes 28
  6.5 142.4 %all-gather.3.cloned.1.call-start = ((), (), s32[]{:S(2)}) async-start(), calls=%async_computation.6 | async-start | bytes 4718592 | tf_op jit(solution)/shard_map/all_gather | solution.py:138
  9.0 81.6 %copy-start = (s32[128]{0:T(128)}, s32[128]{0:T(128)S(1)}, u32[]{:S(2)}) copy-start(s32[128]{0:T(128)S(1)} %fusion.26) | copy-start | bytes 1540
  39.9 113.8 %all-gather.5.cloned.1.call-start = ((), (), s32[]{:S(2)}) async-start(), calls=%async_computation.7 | async-start | bytes 4718592 | tf_op jit(solution)/shard_map/all_gather | solution.py:139
  65.7 14.1 %all-to-all-start = ((s32[32,1,8]{2,1,0:T(1,128)}), s32[32,1,8]{2,1,0:T(1,128)S(1)}, u32[]{:S(2)}, u32[]{:S(2)}) async-start(s32[32,1,8]{2,1,0:T(1,128)} %bitcast.17), calls=%async_computation | async-start | bytes 32768 | tf_op jit(solution)/shard_map/all_to_all | solution.py:127
  81.7 9.7 %all-to-all-start.1 = ((s32[8,1,256]{2,1,0:T(1,128)}), s32[8,1,256]{2,1,0:T(1,128)S(1)}, u32[]{:S(2)}, u32[]{:S(2)}) async-start(s32[8,1,256]{2,1,0:T(1,128)} %stack.6), calls=%async_computation.1 | async-start | bytes 16384 | tf_op jit(solution)/shard_map/all_to_all | solution.py:141
  91.4 54.9 %all-to-all-start.2 = ((bf16[32,8,4096]{2,1,0:T(8,128)(2,1)}), bf16[32,8,4096]{2,1,0:T(8,128)(2,1)S(1)}, u32[]{:S(2)}, u32[]{:S(2)}) async-start(bf16[32,8,4096]{2,1,0:T(8,128)(2,1)} %bitcast.21), calls=%async_computation.2 | async-start | bytes 4194304 | tf_op jit(solution)/shard_map/all_to_all | solution.py:106
  262.6 11.1 %copy-start.1 = (s32[128]{0:T(128)S(1)}, s32[128]{0:T(128)}, u32[]{:S(2)}) copy-start(s32[128]{0:T(128)} %copy-done) | copy-start | bytes 1540
  266.8 55.5 %all-to-all-start.5 = ((bf16[32,8,4096]{2,1,0:T(8,128)(2,1)}), bf16[32,8,4096]{2,1,0:T(8,128)(2,1)S(1)}, u32[]{:S(2)}, u32[]{:S(2)}) async-start(bf16[32,8,4096]{2,1,0:T(8,128)(2,1)} %reshape_reshape_reshape.7), calls=%async_computation.5 | async-start | bytes 4194304 | tf_op jit(solution)/shard_map/all_to_all | solution.py:156
Sparse Core Ops, SparseCore 0:
  40.1 31.3 all-gather.2
  73.3 34.6 all-gather.4
